TPU v7x, 32 devices: a whole 2x2x4 slice. The times are simulated.
32 devices in a mesh: videos: 2 (over x), rows: 16 (over z, y, core).
Axes of the slice: x: 2, y: 2, z: 4, core: 2. Of those that a mesh axis runs over, the one named last changes fastest.
Arguments:
- latents: bfloat16 [4, 32, 64, 384], P('videos', 'rows'), parts along dimension 0, may hold values from -6 to 6
- conv_cache: bfloat16 [4, 32, 64, 384], P('videos', 'rows'), parts along dimension 0, may hold values from -4 to 4
- norm_gain: float32 [384], replicated, may hold values from 0.1 to 1.9
- conv_weight: bfloat16 [3, 3, 3, 384, 384], replicated, may hold values from -0.0625 to 0.0625
- attn_gain: float32 [384], replicated, may hold values from 0.1 to 1.9
- query_weight: bfloat16 [384, 384], replicated, may hold values from -3 to 3
- key_weight: bfloat16 [384, 384], replicated, may hold values from -3 to 3
- value_weight: bfloat16 [384, 384], replicated, may hold values from -0.3125 to 0.3125
- out_weight: bfloat16 [384, 384], replicated, may hold values from -0.3125 to 0.3125
- up_weight: bfloat16 [3, 3, 384, 192], replicated, may hold values from -0.109375 to 0.109375
Outputs:
- decoded: bfloat16 [4, 64, 128, 192], P('videos', 'rows'), parts along dimension 0
- next_cache: bfloat16 [4, 32, 64, 384], P('videos', 'rows'), parts along dimension 0
There are 2 independent parts, one for each index of `videos`. A program takes and returns all parts, laid end to end along the dimension named above; an argument that names none is the same for every part. Nothing has to cross between parts.
All inputs are finite; a program needn't handle non-finite values.
Results may differ from a plain program's by a relative error of at most 0.0058.
Values may be sent and summed in bfloat16 or wider, within the bound.
A program may use at most 128 MiB of HBM per device.

v0:
```python
import jax
import jax.numpy as jnp
from jax import lax
from jax.sharding import PartitionSpec as P


def with_halo(block, sides, width):
    for axis, dim in sides:
        count = lax.axis_size(axis)
        forward = [(i, i + 1) for i in range(count - 1)]
        backward = [(target, source) for source, target in forward]
        low = lax.ppermute(
            lax.slice_in_dim(block, block.shape[dim] - width, None, axis=dim), axis, forward
        )
        high = lax.ppermute(lax.slice_in_dim(block, 0, width, axis=dim), axis, backward)
        block = jnp.concatenate([low, block, high], axis=dim)
    return block


def normalize(values, gain):
    return values * lax.rsqrt(jnp.mean(values * values, axis=-1, keepdims=True) + 1e-06) * gain


def project(rows_in, weight):
    return jnp.dot(rows_in, weight, preferred_element_type=jnp.float32).astype(jnp.bfloat16)


def shards(
    latents,
    conv_cache,
    norm_gain,
    conv_weight,
    attn_gain,
    query_weight,
    key_weight,
    value_weight,
    out_weight,
    up_weight,
):
    frames, rows_here, width, channels = latents.shape
    outputs = up_weight.shape[3]
    values_in = latents.astype(jnp.float32)
    conv_input = jax.nn.silu(normalize(values_in, norm_gain)).astype(jnp.bfloat16)
    stacked = jnp.concatenate([conv_cache, conv_input], axis=0)
    bordered = with_halo(stacked, (("rows", 1),), 1)
    padded = jnp.pad(bordered, ((0, 0), (0, 0), (1, 1), (0, 0)))
    windows = []
    for tap_time in range(3):
        for tap_row in range(3):
            for tap_col in range(3):
                windows.append(
                    padded[
                        tap_time : tap_time + frames,
                        tap_row : tap_row + rows_here,
                        tap_col : tap_col + width,
                    ]
                )
    columns = jnp.concatenate(windows, axis=-1).reshape(-1, 27 * channels)
    conv_out = jnp.dot(
        columns, conv_weight.reshape(27 * channels, channels), preferred_element_type=jnp.float32
    )
    resid = values_in + conv_out.reshape(frames, rows_here, width, channels)
    normed = normalize(resid, attn_gain).astype(jnp.bfloat16)
    flat_normed = normed.reshape(-1, channels)
    queries = project(flat_normed, query_weight).reshape(frames, rows_here * width, channels)
    scale = channels ** (-0.5)
    count = rows_here * width
    piece = lax.all_gather(normed, "rows", axis=1, tiled=True)
    span = piece.shape[1] * piece.shape[2]
    flat_piece = piece.reshape(-1, channels)
    key_piece = project(flat_piece, key_weight).reshape(frames, span, channels)
    value_piece = project(flat_piece, value_weight).reshape(frames, span, channels)
    running_max = jnp.full((frames, count), -1e30, jnp.float32)
    scores = (
        jnp.einsum("fqc,fkc->fqk", queries, key_piece, preferred_element_type=jnp.float32) * scale
    )
    new_max = jnp.maximum(running_max, jnp.max(scores, axis=-1))
    weights = jnp.exp(scores - new_max[..., None])
    new_sum = jnp.sum(weights, axis=-1)
    added = jnp.einsum(
        "fqk,fkc->fqc",
        weights.astype(jnp.bfloat16),
        value_piece,
        preferred_element_type=jnp.float32,
    )
    attended = (added / new_sum[..., None]).astype(jnp.bfloat16)
    projected = jnp.dot(
        attended.reshape(-1, channels), out_weight, preferred_element_type=jnp.float32
    )
    mid = (resid + projected.reshape(frames, rows_here, width, channels)).astype(jnp.bfloat16)
    doubled = jnp.repeat(jnp.repeat(mid, 2, axis=1), 2, axis=2)
    fine_rows = with_halo(doubled, (("rows", 1),), 1)
    fine_pad = jnp.pad(fine_rows, ((0, 0), (0, 0), (1, 1), (0, 0)))
    fine_windows = []
    for tap_row in range(3):
        for tap_col in range(3):
            fine_windows.append(
                fine_pad[:, tap_row : tap_row + 2 * rows_here, tap_col : tap_col + 2 * width]
            )
    fine_columns = jnp.concatenate(fine_windows, axis=-1).reshape(-1, 9 * channels)
    result = jnp.dot(
        fine_columns, up_weight.reshape(9 * channels, outputs), preferred_element_type=jnp.float32
    )
    decoded = result.reshape(frames, 2 * rows_here, 2 * width, outputs).astype(jnp.bfloat16)
    return (decoded, conv_input)


def solution(mesh):
    return jax.shard_map(
        shards,
        mesh=mesh,
        in_specs=(
            P("videos", "rows", None, None),
            P("videos", "rows", None, None),
            P(),
            P(),
            P(),
            P(),
            P(),
            P(),
            P(),
            P(),
        ),
        out_specs=(P("videos", "rows", None, None), P("videos", "rows", None, None)),
        check_vma=False,
    )
```

profile of v0, /device:TPU:1, one launch (start us, length us, event | category | flops | bytes accessed | tf_op | source)
XLA Modules:
  0.0 109.6 jit_solution(16207955762720547455)
XLA Ops:
  7.2 1.1 %fusion.23 = f32[2,2,64]{2,1,0:T(2,128)S(1)} fusion(bf16[2,2,64,384]{3,2,1,0:T(8,128)(2,1)} %param.10), kind=kLoop, calls=%fused_computation.50 | loop fusion | flops 294656 | bytes 197632 | tf_op jit(solution)/shard_map/reduce_sum | solution.py:21
  8.4 1.1 %fusion.30 = bf16[2,2,64,384]{3,2,1,0:T(8,128)(2,1)S(1)} fusion(bf16[2,2,64,384]{3,2,1,0:T(8,128)(2,1)} %param.10, f32[384]{0:T(512)} %param.12, f32[2,2,64]{2,1,0:T(2,128)S(1)} %add_rsqrt_fusion.1), kind=kLoop, calls=%fused_computation.57 | loop fusion | flops 786432 | bytes 395776 | tf_op jit(solution)/shard_map/convert_element_type | solution.py:43
  9.5 1.1 %fusion.33 = (bf16[4,1,64,384]{3,2,1,0:T(8,128)(2,1)S(1)}, bf16[4,1,64,384]{3,2,1,0:T(8,128)(2,1)S(1)}) fusion(bf16[2,2,64,384]{3,2,1,0:T(8,128)(2,1)} %param.11, bf16[2,2,64,384]{3,2,1,0:T(8,128)(2,1)S(1)} %fusion.30), kind=kLoop, calls=%fused_computation.62 | loop fusion | flops 196608 | bytes 786432 | tf_op jit(solution)/shard_map/concatenate | solution.py:44
  10.7 4.7 %collective-permute-start = (bf16[4,1,64,384]{3,2,1,0:T(8,128)(2,1)S(1)}, bf16[4,1,64,384]{3,2,1,0:T(8,128)(2,1)S(1)}, u32[]{:S(2)}, u32[]{:S(2)}) collective-permute-start(bf16[4,1,64,384]{3,2,1,0:T(8,128)(2,1)S(1)} %get-tuple-element.6), channel_id=1, source_target_pairs={{0,1},{1,2},{2,3},{3,4},{4,5},{5,6},{6,7},{7,8},{8,9},{9,10},{10,1... | collective-permute-start | bytes 589832 | tf_op jit(solution)/shard_map/ppermute | solution.py:12
  15.4 1.9 %collective-permute-start.1 = (bf16[4,1,64,384]{3,2,1,0:T(8,128)(2,1)S(1)}, bf16[4,1,64,384]{3,2,1,0:T(8,128)(2,1)S(1)}, u32[]{:S(2)}, u32[]{:S(2)}) collective-permute-start(bf16[4,1,64,384]{3,2,1,0:T(8,128)(2,1)S(1)} %get-tuple-element.7), channel_id=1, source_target_pairs={{1,0},{2,1},{3,2},{4,3},{5,4},{6,5},{7,6},{8,7},{9,8},{10,9},{11,1... | collective-permute-start | bytes 589832 | tf_op jit(solution)/shard_map/ppermute | solution.py:15
  17.3 0.7 collective-permute-done
  17.9 4.4 %collective-permute-done.1 = bf16[4,1,64,384]{3,2,1,0:T(8,128)(2,1)S(1)} collective-permute-done((bf16[4,1,64,384]{3,2,1,0:T(8,128)(2,1)S(1)}, bf16[4,1,64,384]{3,2,1,0:T(8,128)(2,1)S(1)}, u32[]{:S(2)}, u32[]{:S(2)}) %collective-permute-start.1) | collective-permute-done | bytes 196640 | tf_op jit(solution)/shard_map/ppermute | solution.py:15
  22.3 1.3 %select_maximum_fusion = bf16[4,4,66,384]{3,2,1,0:T(8,128)(2,1)S(1)} fusion(bf16[4,1,64,384]{3,2,1,0:T(8,128)(2,1)S(1)} %collective-permute-done.1, bf16[4,1,64,384]{3,2,1,0:T(8,128)(2,1)S(1)} %collective-permute-done, bf16[2,2,64,384]{3,2,1,0:T(8,128)(2,1)S(1)} %fusion.30, bf16[2,2,64,384]{3,2,1,0:T(8,128)(2,1)} %param.11), kind=kLoop, calls=%fused_computation.27 | loop fusion | flops 6082560 | bytes 1597440 | tf_op jit(solution)/shard_map/concatenate | solution.py:16
  23.6 1.2 %pad_maximum_fusion.2 = (bf16[4,3,64,384]{3,2,1,0:T(8,128)(2,1)S(1)}, bf16[4,3,64,384]{3,2,1,0:T(8,128)(2,1)S(1)}) fusion(bf16[4,1,64,384]{3,2,1,0:T(8,128)(2,1)S(1)} %collective-permute-done.1, bf16[2,2,64,384]{3,2,1,0:T(8,128)(2,1)S(1)} %fusion.30, bf16[2,2,64,384]{3,2,1,0:T(8,128)(2,1)} %param.11, bf16[4,1,64,384]{3,2,1,0:T(8,128)(2,1)S(1)} %collective-permute-done), kind=kLoop, calls=%fused_computation.45 | loop fusion | flops 1179648 | bytes 1966080 | tf_op jit(solution)/shard_map/concatenate | solution.py:16
  26.4 0.9 slice-done.1
  27.3 3.0 %multiply_reduce_fusion = (f32[2,2,64]{2,1,0:T(2,128)S(1)}, f32[2,2,64,384]{3,2,1,0:T(8,128)S(1)}) fusion(bf16[2,2,64,10368]{3,2,1,0:T(8,128)(2,1)S(1)} %slice_dynamic-update-slice_fusion.6, bf16[10368,384,1,1]{1,0,3,2:T(8,128)(2,1)S(1)} %bitcast.47, bf16[2,2,64,384]{3,2,1,0:T(8,128)(2,1)S(1)} %copy-done.4), kind=kOutput, calls=%fused_computation.59 | convolution fusion | flops 2038824704 | bytes 13861888 | tf_op jit(solution)/shard_map/dot_general | solution.py:59
  30.3 0.8 multiply_convert_fusion
  31.1 1.2 %convolution_convert_fusion.2 = bf16[256,384]{1,0:T(8,128)(2,1)S(1)} fusion(bf16[256,384]{1,0:T(8,128)(2,1)} %bitcast.41, bf16[384,384]{1,0:T(8,128)(2,1)S(1)} %copy-done.7), kind=kOutput, calls=%fused_computation.23 | convolution fusion | flops 75595776 | bytes 688128 | tf_op jit(solution)/shard_map/dot_general | solution.py:25
  32.4 45.2 %all-gather.2.cloned.1.call-done = bf16[2,32,64,384]{3,2,1,0:T(8,128)(2,1)} async-done(((bf16[2,2,64,384]{3,2,1,0:T(8,128)(2,1)}), bf16[2,32,64,384]{3,2,1,0:T(8,128)(2,1)}) %all-gather.2.cloned.1.call-update) | async-done | bytes 3145744 | tf_op jit(solution)/shard_map/all_gather | solution.py:68
  77.6 4.1 %convolution_convert_fusion.1 = bf16[4096,384]{1,0:T(8,128)(2,1)S(1)} fusion(bf16[4096,384]{1,0:T(8,128)(2,1)} %bitcast.37, bf16[384,384]{1,0:T(8,128)(2,1)S(1)} %copy-done), kind=kOutput, calls=%fused_computation.1 | convolution fusion | flops 1209532416 | bytes 6586368 | tf_op jit(solution)/shard_map/dot_general | solution.py:25
  81.7 1.2 %fusion.36 = (f32[2,128]{1,0:T(2,128)S(1)}, f32[2,128,2048]{2,1,0:T(8,128)S(1)}) fusion(bf16[2,128,384]{2,1,0:T(8,128)(2,1)S(1)} %bitcast.43, bf16[2,2048,384]{2,1,0:T(8,128)(2,1)S(1)} %bitcast.39), kind=kOutput, calls=%fused_computation.96 | convolution fusion | flops 403701504 | bytes 5440512 | tf_op jit(solution)/shard_map/fqc,fkc->fqk/dot_general | solution.py:75
  82.9 2.1 %convolution_convert_fusion = bf16[4096,384]{1,0:T(8,128)(2,1)S(1)} fusion(bf16[4096,384]{1,0:T(8,128)(2,1)S(1)} %bitcast.38, bf16[384,384]{1,0:T(8,128)(2,1)S(1)} %copy-done.6), kind=kOutput, calls=%fused_computation | convolution fusion | flops 1209532416 | bytes 6586368 | tf_op jit(solution)/shard_map/dot_general | solution.py:25
  85.4 0.8 fusion.14
  87.4 0.7 fusion.35
  88.2 2.3 %collective-permute-start.2 = (bf16[2,1,128,384]{3,2,1,0:T(8,128)(2,1)}, bf16[2,1,128,384]{3,2,1,0:T(8,128)(2,1)S(1)}, u32[]{:S(2)}, u32[]{:S(2)}) collective-permute-start(bf16[2,1,128,384]{3,2,1,0:T(8,128)(2,1)} %get-tuple-element.2), channel_id=1, source_target_pairs={{0,1},{1,2},{2,3},{3,4},{4,5},{5,6},{6,7},{7,8},{8,9},{9,10},{10,1... | collective-permute-start | bytes 589832 | tf_op jit(solution)/shard_map/ppermute | solution.py:12
  90.5 2.0 %collective-permute-start.3 = (bf16[2,1,128,384]{3,2,1,0:T(8,128)(2,1)S(1)}, bf16[2,1,128,384]{3,2,1,0:T(8,128)(2,1)S(1)}, u32[]{:S(2)}, u32[]{:S(2)}) collective-permute-start(bf16[2,1,128,384]{3,2,1,0:T(8,128)(2,1)S(1)} %get-tuple-element.3), channel_id=1, source_target_pairs={{1,0},{2,1},{3,2},{4,3},{5,4},{6,5},{7,6},{8,7},{9,8},{10,9},{11,1... | collective-permute-start | bytes 589832 | tf_op jit(solution)/shard_map/ppermute | solution.py:15
  92.5 2.5 %copy.12 = bf16[3,3,384,192]{2,1,0,3:T(4,128)(2,1)S(1)} copy(bf16[3,3,384,192]{2,3,1,0:T(8,128)(2,1)} %param.19) | data formatting | bytes 2654208 | tf_op args[9]
  95.0 2.4 %reshape.76 = bf16[3456,192,1,1]{0,1,2,3:T(8,128)(2,1)} reshape(bf16[3,3,384,192]{2,1,0,3:T(4,128)(2,1)S(1)} %copy.12) | data formatting | bytes 2654208 | tf_op jit(solution)/shard_map/reshape | solution.py:102
  99.6 3.2 %fusion.11 = bf16[2,4,128,192]{2,3,1,0:T(8,128)(2,1)} fusion(bf16[2,4,128,3456]{3,2,1,0:T(8,128)(2,1)S(1)} %slice_dynamic-update-slice_fusion, bf16[3456,192,1,1]{0,1,2,3:T(8,128)(2,1)S(1)} %copy-done.5), kind=kOutput, calls=%fused_computation.19 | convolution fusion | flops 1359151104 | bytes 8798208 | tf_op jit(solution)/shard_map/dot_general | solution.py:101
  (75 shorter events, 5.3 us)
Async XLA Ops:
  7.2 70.4 %copy-start = (bf16[384,384]{1,0:T(8,128)(2,1)S(1)}, bf16[384,384]{1,0:T(8,128)(2,1)}, u32[]{:S(2)}) copy-start(bf16[384,384]{1,0:T(8,128)(2,1)} %param.16) | copy-start | bytes 884740
  7.2 17.8 %copy-start.2 = (bf16[2,2,64,384]{3,2,1,0:T(8,128)(2,1)S(1)}, bf16[2,2,64,384]{3,2,1,0:T(8,128)(2,1)}, u32[]{:S(2)}) copy-start(bf16[2,2,64,384]{3,2,1,0:T(8,128)(2,1)} %param.11) | copy-start | bytes 589828
  7.2 70.4 %all-gather.2.cloned.1.call-start = ((), (), s32[]{:S(2)}) async-start(), calls=%async_computation | async-start | bytes 3342336 | tf_op jit(solution)/shard_map/all_gather | solution.py:68
  9.5 16.1 %copy-start.3 = (bf16[2,2,64,384]{3,2,1,0:T(8,128)(2,1)}, bf16[2,2,64,384]{3,2,1,0:T(8,128)(2,1)S(1)}, u32[]{:S(2)}) copy-start(bf16[2,2,64,384]{3,2,1,0:T(8,128)(2,1)S(1)} %fusion.30) | copy-start | bytes 589828
  9.5 16.9 %slice-start = ((s8[7962624]{0:T(1024)(128)(4,1)}), s8[4194304]{0:T(1024)(128)(4,1)S(1)}, s32[]{:S(2)}) async-start(s8[7962624]{0:T(1024)(128)(4,1)} %bitcast.45), calls=%async_computation.1 | async-start | bytes 8388608
  10.7 7.3 %collective-permute-start = (bf16[4,1,64,384]{3,2,1,0:T(8,128)(2,1)S(1)}, bf16[4,1,64,384]{3,2,1,0:T(8,128)(2,1)S(1)}, u32[]{:S(2)}, u32[]{:S(2)}) collective-permute-start(bf16[4,1,64,384]{3,2,1,0:T(8,128)(2,1)S(1)} %get-tuple-element.6), channel_id=1, source_target_pairs={{0,1},{1,2},{2,3},{3,4},{4,5},{5,6},{6,7},{7,8},{8,9},{9,10},{10,1... | collective-permute-start | bytes 589832 | tf_op jit(solution)/shard_map/ppermute | solution.py:12
  15.4 7.0 %collective-permute-start.1 = (bf16[4,1,64,384]{3,2,1,0:T(8,128)(2,1)S(1)}, bf16[4,1,64,384]{3,2,1,0:T(8,128)(2,1)S(1)}, u32[]{:S(2)}, u32[]{:S(2)}) collective-permute-start(bf16[4,1,64,384]{3,2,1,0:T(8,128)(2,1)S(1)} %get-tuple-element.7), channel_id=1, source_target_pairs={{1,0},{2,1},{3,2},{4,3},{5,4},{6,5},{7,6},{8,7},{9,8},{10,9},{11,1... | collective-permute-start | bytes 589832 | tf_op jit(solution)/shard_map/ppermute | solution.py:15
  23.6 2.3 %copy-start.4 = (bf16[2,2,64,384]{3,2,1,0:T(8,128)(2,1)S(1)}, bf16[2,2,64,384]{3,2,1,0:T(8,128)(2,1)}, u32[]{:S(2)}) copy-start(bf16[2,2,64,384]{3,2,1,0:T(8,128)(2,1)} %param.10) | copy-start | bytes 589828
  23.6 2.3 %copy-start.9 = (f32[384]{0:T(512)S(1)}, f32[384]{0:T(512)}, u32[]{:S(2)}) copy-start(f32[384]{0:T(512)} %param.12) | copy-start | bytes 4612
  25.2 2.1 %slice-start.1 = ((s8[7962624]{0:T(1024)(128)(4,1)}), s8[3768320]{0:T(1024)(128)(4,1)S(1)}, s32[]{:S(2)}) async-start(s8[7962624]{0:T(1024)(128)(4,1)} %bitcast.45), calls=%async_computation.2 | async-start | bytes 7536640
  27.3 3.0 %copy-start.10 = (f32[384]{0:T(512)S(1)}, f32[384]{0:T(512)}, u32[]{:S(2)}) copy-start(f32[384]{0:T(512)} %param.14) | copy-start | bytes 4612
  27.3 3.9 %copy-start.7 = (bf16[384,384]{1,0:T(8,128)(2,1)S(1)}, bf16[384,384]{1,0:T(8,128)(2,1)}, u32[]{:S(2)}) copy-start(bf16[384,384]{1,0:T(8,128)(2,1)} %param.15) | copy-start | bytes 884740
  77.6 5.3 %copy-start.1 = (bf16[2,32,64,384]{3,2,1,0:T(8,128)(2,1)S(1)}, bf16[2,32,64,384]{3,2,1,0:T(8,128)(2,1)}, u32[]{:S(2)}) copy-start(bf16[2,32,64,384]{3,2,1,0:T(8,128)(2,1)} %all-gather.2.cloned.1.call-done) | copy-start | bytes 9437188
  77.6 5.3 %copy-start.6 = (bf16[384,384]{1,0:T(8,128)(2,1)S(1)}, bf16[384,384]{1,0:T(8,128)(2,1)}, u32[]{:S(2)}) copy-start(bf16[384,384]{1,0:T(8,128)(2,1)} %param.17) | copy-start | bytes 884740
  85.0 1.2 %copy-start.8 = (bf16[384,384]{1,0:T(8,128)(2,1)S(1)}, bf16[384,384]{1,0:T(8,128)(2,1)}, u32[]{:S(2)}) copy-start(bf16[384,384]{1,0:T(8,128)(2,1)} %param.18) | copy-start | bytes 884740
  88.2 9.2 %collective-permute-start.2 = (bf16[2,1,128,384]{3,2,1,0:T(8,128)(2,1)}, bf16[2,1,128,384]{3,2,1,0:T(8,128)(2,1)S(1)}, u32[]{:S(2)}, u32[]{:S(2)}) collective-permute-start(bf16[2,1,128,384]{3,2,1,0:T(8,128)(2,1)} %get-tuple-element.2), channel_id=1, source_target_pairs={{0,1},{1,2},{2,3},{3,4},{4,5},{5,6},{6,7},{7,8},{8,9},{9,10},{10,1... | collective-permute-start | bytes 589832 | tf_op jit(solution)/shard_map/ppermute | solution.py:12
  90.5 7.0 %collective-permute-start.3 = (bf16[2,1,128,384]{3,2,1,0:T(8,128)(2,1)S(1)}, bf16[2,1,128,384]{3,2,1,0:T(8,128)(2,1)S(1)}, u32[]{:S(2)}, u32[]{:S(2)}) collective-permute-start(bf16[2,1,128,384]{3,2,1,0:T(8,128)(2,1)S(1)} %get-tuple-element.3), channel_id=1, source_target_pairs={{1,0},{2,1},{3,2},{4,3},{5,4},{6,5},{7,6},{8,7},{9,8},{10,9},{11,1... | collective-permute-start | bytes 589832 | tf_op jit(solution)/shard_map/ppermute | solution.py:15
  98.1 1.5 %copy-start.5 = (bf16[3456,192,1,1]{0,1,2,3:T(8,128)(2,1)S(1)}, bf16[3456,192,1,1]{0,1,2,3:T(8,128)(2,1)}, u32[]{:S(2)}) copy-start(bf16[3456,192,1,1]{0,1,2,3:T(8,128)(2,1)} %reshape.76) | copy-start | bytes 3981316
Sparse Core Ops, SparseCore 0:
  31.3 46.2 all-gather.1
where the time goes:
time: 111 us; the launch traced here: 110 us
  waiting for transfers between devices  50.4 us (45%)
  matrix products  15.9 us (14%)
  between operations  14.5 us (13%)
  starting transfers between devices  10.9 us (10%)
  local copies, waits for them, and re-layouts  9.88 us (9%)
  other arithmetic  7.95 us (7%)
    all_gather x1, waiting for transfers between devices, shards(): piece = lax.all_gather(normed, 'rows', axis=1, tiled=True)  45.2 us
    dot_general x3, matrix products, project(): jnp.dot(rows_in, weight, preferred_element_type=jnp.float32)  7.38 us
    ppermute x2, starting transfers between devices, with_halo(): lax.ppermute(lax.slice_in_dim(block, block.shape[dim] - width, None, axis...  6.98 us
    unnamed x57, local copies, waits for them, and re-layouts  5.56 us
    ppermute x2, waiting for transfers between devices, with_halo(): lax.ppermute(lax.slice_in_dim(block, 0, width, axis=dim), axis, backward)  4.54 us
    ppermute x2, starting transfers between devices, with_halo(): lax.ppermute(lax.slice_in_dim(block, 0, width, axis=dim), axis, backward)  3.93 us
    dot_general x1, matrix products, shards(): jnp.dot(fine_columns, up_weight.reshape(9 * channels, outputs), preferred...  3.2 us
    dot_general x1, matrix products, shards(): jnp.dot(columns, conv_weight.reshape(27 * channels, channels), preferred_...  3.03 us
  transfers between devices with their start and end apart: 5, of which 4 were waited for; matrix products, arithmetic and copies ran while one was open for 5% of the time, Pallas kernels for 0%

commit v1 on v0

v1 whole, which is shorter than its diff:
```python
import functools

import jax
import jax.numpy as jnp
from jax import lax
from jax.experimental import pallas as pl
from jax.experimental.pallas import tpu as pltpu
from jax.sharding import PartitionSpec as P

F32, BF16 = jnp.float32, jnp.bfloat16


def normalize(values, gain):
    return values * lax.rsqrt(jnp.mean(values * values, axis=-1, keepdims=True) + 1e-06) * gain


def with_columns(flat, width):
    values = flat.astype(F32)
    n = values.shape[0]
    column = lax.rem(lax.broadcasted_iota(jnp.int32, values.shape, 0), width)
    left = jnp.where(column == 0, 0.0, pltpu.roll(values, 1, 0)).astype(BF16)
    right = jnp.where(column == width - 1, 0.0, pltpu.roll(values, n - 1, 0)).astype(BF16)
    return jnp.concatenate([left, flat, right], axis=-1)


def dot_nt(a, b):
    return lax.dot_general(a, b, (((1,), (1,)), ((), ())), preferred_element_type=F32)


def dot(a, b):
    return jnp.dot(a, b, preferred_element_type=F32)


def kernel(
    nz, ny,
    latents, cache, gain, attn_gain, conv_hbm, q_hbm, k_hbm, v_hbm, o_hbm, up_hbm,
    decoded, next_cache,
    conv_w, q_w, k_w, v_w, o_w, up_w, up_p,
    lat, stk, ext, ext3, resid, keys, query, top, total, acc, mid, midx, mid3,
    w_sem, a_send, a_recv, z_send, z_recv, y_send, y_recv, c_send, c_recv,
):
    _, rows, width, channels = latents.shape
    band = 2 * rows
    outputs = decoded.shape[3]
    me = lax.axis_index("rows")
    chip, core = me // 2, me % 2
    z, y = chip // ny, chip % ny
    chips = nz * ny
    sibling = me + 1 - 2 * core
    has_prev, has_next = chip > 0, chip < chips - 1

    weights = [
        pltpu.make_async_copy(conv_hbm.at[pl.ds(3 * i, 3)], conv_w.at[pl.ds(3 * i, 3)], w_sem.at[i])
        for i in range(3)
    ]
    for i, (source, target) in enumerate(
        ((q_hbm, q_w), (k_hbm, k_w), (v_hbm, v_w), (o_hbm, o_w), (up_hbm, up_w))
    ):
        weights.append(pltpu.make_async_copy(source, target, w_sem.at[3 + i]))
    for copy in weights:
        copy.start()

    barrier = pltpu.get_barrier_semaphore()

    def greet(device):
        pl.semaphore_signal(
            barrier, inc=1, device_id={"rows": device}, device_id_type=pl.DeviceIdType.MESH
        )

    greet(sibling)
    met = 1

    @pl.when(has_prev)
    def _():
        greet(2 * chip - 2)
        greet(2 * chip - 1)

    @pl.when(has_next)
    def _():
        greet(2 * chip + 2)
        greet(2 * chip + 3)

    met = met + 2 * has_prev.astype(jnp.int32) + 2 * has_next.astype(jnp.int32)
    if ny > 1:

        @pl.when(z > 0)
        def _():
            greet(me - 2 * ny)

        @pl.when(z < nz - 1)
        def _():
            greet(me + 2 * ny)

        met = met + (z > 0).astype(jnp.int32) + (z < nz - 1).astype(jnp.int32)

    def remote(source, target, send, recv, device):
        return pltpu.make_async_remote_copy(
            src_ref=source,
            dst_ref=target,
            send_sem=send,
            recv_sem=recv,
            device_id={"rows": device},
            device_id_type=pl.DeviceIdType.MESH,
        )

    values_in = latents[...].astype(F32)
    normal = normalize(values_in, gain[...].reshape(1, 1, 1, channels))
    conv_input = (normal / (1.0 + jnp.exp(-normal))).astype(BF16)
    next_cache[...] = conv_input
    stk[0:2] = cache[...]
    stk[2:4] = conv_input

    pl.semaphore_wait(barrier, met)

    def halo(group, first, count, slot, source_row, target_row, device, kind):
        return remote(
            stk.at[pl.ds(group + first, count), pl.ds(source_row, 1)],
            ext.at[pl.ds(first, count), pl.ds(target_row, 1)],
            a_send.at[slot],
            a_recv.at[kind],
            device,
        )

    other = 1 - core
    to_sibling = [
        remote(
            stk.at[pl.ds(other + first, count)],
            ext.at[pl.ds(first, count), pl.ds(1 + rows * core, rows)],
            a_send.at[slot],
            a_recv.at[slot],
            sibling,
        )
        for slot, (first, count) in enumerate(((0, 1), (1, 2)))
    ]
    to_sibling.append(
        remote(
            latents.at[other], lat.at[pl.ds(rows * core, rows)], a_send.at[2], a_recv.at[2], sibling
        )
    )
    up_halo, down_halo = [], []
    for step, (first, count) in enumerate(((0, 1), (1, 2))):
        for g in range(2):
            slot = 3 + 2 * step + g
            down_halo.append(
                halo(g, first, count, slot, rows - 1, 0, 2 * chip + 2 + g, 3 + step)
            )
            up_halo.append(halo(g, first, count, slot, 0, band + 1, 2 * chip - 2 + g, 5 + step))
    sends_down = (core == 1) & has_next
    sends_up = (core == 0) & has_prev

    @pl.when(sends_down)
    def _():
        for copy in down_halo:
            copy.start()

    @pl.when(sends_up)
    def _():
        for copy in up_halo:
            copy.start()

    for copy in to_sibling:
        copy.start()

    ext[:, pl.ds(1 + rows * core, rows)] = stk[pl.ds(core, 3)]
    lat[pl.ds(rows * core, rows)] = latents[core]
    edge = jnp.zeros((3, 1, width, channels), BF16)

    @pl.when(jnp.logical_not(has_prev))
    def _():
        ext[:, 0:1] = edge

    @pl.when(jnp.logical_not(has_next))
    def _():
        ext[:, band + 1 : band + 2] = edge

    def arrived(target, sem):
        remote(target, target, a_send.at[0], sem, sibling).wait_recv()

    conv_out = jnp.zeros((band * width, channels), F32)
    for i in range(3):
        if i < 2:
            first, count = ((0, 1), (1, 2))[i]
            arrived(ext.at[pl.ds(first, count), pl.ds(1 + rows * other, rows)], a_recv.at[i])

            @pl.when(has_prev)
            def _():
                arrived(ext.at[pl.ds(first, count), pl.ds(0, 1)], a_recv.at[3 + i])

            @pl.when(has_next)
            def _():
                arrived(ext.at[pl.ds(first, count), pl.ds(band + 1, 1)], a_recv.at[5 + i])

        flat = ext[i].reshape((band + 2) * width, channels)
        ext3[i] = with_columns(flat, width)
        weights[i].wait()
        for j in range(3):
            window = ext3[i, j * width : (j + band) * width]
            conv_out = conv_out + dot(window, conv_w[3 * i + j])

    arrived(lat.at[pl.ds(rows * other, rows)], a_recv.at[2])
    resid_now = lat[...].reshape(band * width, channels).astype(F32) + conv_out
    resid[...] = resid_now
    normed = normalize(resid_now, attn_gain[...]).astype(BF16)
    keys[chip] = normed

    def up(block):
        index = block * ny + y
        return remote(
            keys.at[index], keys.at[index], z_send.at[block], z_recv.at[block], me + 2 * ny
        )

    def down(block):
        index = block * ny + y
        return remote(
            keys.at[index], keys.at[index], z_send.at[nz + block], z_recv.at[block], me - 2 * ny
        )

    def across(block):
        index = block * ny + y
        return remote(
            keys.at[index],
            keys.at[index],
            y_send.at[block],
            y_recv.at[block],
            me + 2 * (1 - 2 * y),
        )

    @pl.when(z < nz - 1)
    def _():
        up(z).start()

    @pl.when(z > 0)
    def _():
        down(z).start()

    if ny > 1:
        across(z).start()

    for copy in weights[3:]:
        copy.wait()
    queries = dot(normed, q_w[...]).astype(BF16)
    query[...] = (dot_nt(queries, k_w[...]) * channels ** (-0.5)).astype(BF16)

    scores = dot_nt(query[...], normed)
    largest = jnp.max(scores, axis=-1, keepdims=True)
    part = jnp.exp(scores - largest)
    top[...] = largest
    total[...] = jnp.sum(part, axis=-1, keepdims=True)
    acc[...] = dot(part.astype(BF16), normed)

    taps = {(0, 0): (0,), (0, 1): (1, 2), (1, 0): (0, 1), (1, 1): (2,)}
    for a in range(2):
        for t in range(2):
            for l_sets in range(2):
                for u in range(2):
                    summed = None
                    for j in taps[a, t]:
                        for l in taps[l_sets, u]:
                            term = up_w[j, l].astype(F32)
                            summed = term if summed is None else summed + term
                    up_p[a, l_sets, t, u * channels : (u + 1) * channels] = summed.astype(BF16)

    def attend(index):
        block = keys[index]
        scores = dot_nt(query[...], block)
        before = top[...]
        largest = jnp.maximum(before, jnp.max(scores, axis=-1, keepdims=True))
        part = jnp.exp(scores - largest)
        fade = jnp.exp(before - largest)
        top[...] = largest
        total[...] = total[...] * fade + jnp.sum(part, axis=-1, keepdims=True)
        acc[...] = acc[...] * fade + dot(part.astype(BF16), block)

    def z_arrived(block):
        index = block * ny + y
        remote(keys.at[index], keys.at[index], z_send.at[0], z_recv.at[block], sibling).wait_recv()

    def y_arrived(block):
        index = block * ny + 1 - y
        remote(keys.at[index], keys.at[index], y_send.at[0], y_recv.at[block], sibling).wait_recv()

    def gather_step(d, carry):
        low, high = z - d, z + d

        @pl.when(low >= 0)
        def _():
            z_arrived(low)

            @pl.when(z < nz - 1)
            def _():
                up(low).start()

            if ny > 1:
                across(low).start()

        @pl.when(high < nz)
        def _():
            z_arrived(high)

            @pl.when(z > 0)
            def _():
                down(high).start()

            if ny > 1:
                across(high).start()

        @pl.when(low >= 0)
        def _():
            attend(low * ny + y)

        @pl.when(high < nz)
        def _():
            attend(high * ny + y)

        if ny > 1:

            @pl.when(low + 1 >= 0)
            def _():
                y_arrived(low + 1)
                attend((low + 1) * ny + 1 - y)

            @pl.when((high - 1 < nz) & (d > 1))
            def _():
                y_arrived(high - 1)
                attend((high - 1) * ny + 1 - y)

        return carry

    lax.fori_loop(1, nz + 1 if ny > 1 else nz, gather_step, 0)

    mixed = (acc[...] / total[...]).astype(BF16)
    attended = dot(mixed, v_w[...]).astype(BF16)
    mid_now = (resid[...] + dot(attended, o_w[...])).astype(BF16)
    mid[...] = mid_now.reshape(band, width, channels)

    near = rows + 1
    mid_sibling = remote(
        mid.at[pl.ds(other * (rows - 1), near)],
        midx.at[core, pl.ds(core, near)],
        c_send.at[0],
        c_recv.at[0],
        sibling,
    )
    mid_down = remote(
        mid.at[pl.ds(band - 1, 1)],
        midx.at[core, pl.ds(0, 1)],
        c_send.at[1],
        c_recv.at[1 + core],
        2 * chip + 2,
    )
    mid_up = remote(
        mid.at[pl.ds(0, 1)],
        midx.at[core, pl.ds(rows + 1, 1)],
        c_send.at[2],
        c_recv.at[1 + core],
        2 * chip - 1,
    )

    @pl.when(has_next)
    def _():
        mid_down.start()

    @pl.when(has_prev)
    def _():
        mid_up.start()

    mid_sibling.start()
    midx[core, pl.ds(1 - core, near)] = mid[pl.ds(core * (rows - 1), near)]
    has_halo = ((core == 0) & has_prev) | ((core == 1) & has_next)
    edge_row = (rows + 1) * core

    @pl.when(jnp.logical_not(has_halo))
    def _():
        midx[:, pl.ds(edge_row, 1)] = jnp.zeros((2, 1, width, channels), BF16)

    for copy in to_sibling:
        copy.wait_send()

    @pl.when(sends_down)
    def _():
        for copy in down_halo:
            copy.wait_send()

    @pl.when(sends_up)
    def _():
        for copy in up_halo:
            copy.wait_send()

    def sent(block, carry):
        @pl.when((block <= z) & (z < nz - 1))
        def _():
            up(block).wait_send()

        @pl.when((block >= z) & (z > 0))
        def _():
            down(block).wait_send()

        if ny > 1:
            across(block).wait_send()
        return carry

    lax.fori_loop(0, nz, sent, 0)

    target = midx.at[other, pl.ds(core, near)]
    remote(
        midx.at[other, pl.ds(1 - core, near)],
        midx.at[other, pl.ds(1 - core, near)],
        c_send.at[0],
        c_recv.at[0],
        sibling,
    ).wait_recv()

    @pl.when(has_halo)
    def _():
        for f in range(2):
            landed = midx.at[f, pl.ds(edge_row, 1)]
            remote(landed, landed, c_send.at[0], c_recv.at[1 + f], sibling).wait_recv()

    for f in range(2):
        mid3[f] = with_columns(midx[f].reshape((rows + 2) * width, channels), width)

    fine = 2 * width
    at_row = lax.broadcasted_iota(jnp.int32, (fine, fine), 0)
    at_col = lax.broadcasted_iota(jnp.int32, (fine, fine), 1)
    weave = (at_col == (at_row % 2) * width + at_row // 2).astype(F32).astype(BF16)
    for a in range(2):
        sides = []
        for b in range(2):
            result = None
            for t in range(2):
                window = mid3[
                    :, (a + t) * width : (a + t + rows) * width,
                    b * channels : (b + 2) * channels,
                ].reshape(2 * rows * width, 2 * channels)
                term = dot(window, up_p[a, b, t])
                result = term if result is None else result + term
            sides.append(result.astype(BF16).reshape(2, rows, width, outputs))
        for f in range(2):
            for r in range(rows):
                pair = jnp.concatenate([sides[0][f, r], sides[1][f, r]], axis=0)
                decoded[f, 2 * r + a] = dot(weave, pair).astype(BF16)

    mid_sibling.wait_send()

    @pl.when(has_next)
    def _():
        mid_down.wait_send()

    @pl.when(has_prev)
    def _():
        mid_up.wait_send()


def solution(mesh):
    ny = 4 // mesh.shape["videos"]
    nz = mesh.shape["rows"] // (2 * ny)

    def shards(
        latents, conv_cache, norm_gain, conv_weight, attn_gain,
        query_weight, key_weight, value_weight, out_weight, up_weight,
    ):
        frames, rows, width, channels = latents.shape
        outputs = up_weight.shape[3]
        band = 2 * rows
        vmem = pl.BlockSpec(memory_space=pltpu.VMEM)
        hbm = pl.BlockSpec(memory_space=pl.ANY)
        square = pltpu.VMEM((channels, channels), BF16)
        dma = pltpu.SemaphoreType.DMA
        return pl.pallas_call(
            functools.partial(kernel, nz, ny),
            out_shape=(
                jax.ShapeDtypeStruct((frames, 2 * rows, 2 * width, outputs), BF16),
                jax.ShapeDtypeStruct(latents.shape, BF16),
            ),
            in_specs=[vmem] * 4 + [hbm] * 6,
            out_specs=(vmem, vmem),
            scratch_shapes=[
                pltpu.VMEM((9, 3 * channels, channels), BF16),
                square, square, square, square,
                pltpu.VMEM((3, 3, channels, outputs), BF16),
                pltpu.VMEM((2, 2, 2, 2 * channels, outputs), BF16),
                pltpu.VMEM((band, width, channels), BF16),
                pltpu.VMEM((4, rows, width, channels), BF16),
                pltpu.VMEM((3, band + 2, width, channels), BF16),
                pltpu.VMEM((3, (band + 2) * width, 3 * channels), BF16),
                pltpu.VMEM((band * width, channels), F32),
                pltpu.VMEM((nz * ny, band * width, channels), BF16),
                pltpu.VMEM((band * width, channels), BF16),
                pltpu.VMEM((band * width, 1), F32),
                pltpu.VMEM((band * width, 1), F32),
                pltpu.VMEM((band * width, channels), F32),
                pltpu.VMEM((band, width, channels), BF16),
                pltpu.VMEM((2, rows + 2, width, channels), BF16),
                pltpu.VMEM((2, (rows + 2) * width, 3 * channels), BF16),
                dma((8,)), dma((7,)), dma((7,)),
                dma((2 * nz,)), dma((nz,)), dma((nz,)), dma((nz,)),
                dma((3,)), dma((3,)),
            ],
            compiler_params=pltpu.CompilerParams(
                collective_id=0, has_side_effects=True, vmem_limit_bytes=50 * 1024 * 1024
            ),
        )(
            latents, conv_cache,
            norm_gain.reshape(1, channels), attn_gain.reshape(1, channels),
            conv_weight.reshape(9, 3 * channels, channels),
            query_weight, key_weight, value_weight, out_weight, up_weight,
        )

    split = P("videos", "rows", None, None)
    return jax.shard_map(
        shards,
        mesh=mesh,
        in_specs=(split, split) + (P(),) * 8,
        out_specs=(split, split),
        check_vma=False,
    )
```

time: 111 us -> 56.5 us (0.51)
  waiting for transfers between devices: 50.4 us -> 0 us
  Pallas kernels: 0 us -> 46.4 us
  matrix products: 15.9 us -> 0 us
  between operations: 14.5 us -> 0.73 us
  starting transfers between devices: 10.9 us -> 0 us
  other arithmetic: 7.95 us -> 0 us
    pallas_call x0 -> x1, Pallas kernels: none -> 46.4 us  [shards(): pl.pallas_call(functools.partial(kernel, nz, ny), out_shape=(jax.ShapeDty...]
    all_gather x1 -> x0, waiting for transfers between devices: 45.2 us -> none  [shards(): piece = lax.all_gather(normed, 'rows', axis=1, tiled=True)]
    dot_general x8 -> x0, matrix products: 15.9 us -> none  [the longest x3 7.38 us: project(): jnp.dot(rows_in, weight, preferred_element_type=jnp.float32)]
    ppermute x4 -> x0, starting transfers between devices: 10.9 us -> none  [the longest x2 6.98 us: with_halo(): lax.ppermute(lax.slice_in_dim(block, block.shape[dim] - width, None, axis...]
    ppermute x4 -> x0, waiting for transfers between devices: 5.21 us -> none  [the longest x2 4.54 us: with_halo(): lax.ppermute(lax.slice_in_dim(block, 0, width, axis=dim), axis, backward)]
    concatenate x4 -> x0, other arithmetic: 3.92 us -> none  [the longest x3 2.78 us: with_halo(): block = jnp.concatenate([low, block, high], axis=dim)]
    convert_element_type x2 -> x0, other arithmetic: 1.9 us -> none  [the longest x1 1.12 us: shards(): jax.nn.silu(normalize(values_in, norm_gain)).astype(jnp.bfloat16)]
    reduce_sum x2 -> x0, other arithmetic: 1.55 us -> none  [the longest x1 1.12 us: normalize(): jnp.mean(values * values, axis=-1, keepdims=True) + 1e-06]
  transfers between devices with their start and end apart: 5 -> 0, of which waited for: 4 -> 0; matrix products, arithmetic and copies ran while one was open for 5% -> 0% of each run, Pallas kernels for 0% -> 0%
where the time goes in v1:
time: 56.5 us; the launch traced here: 56.2 us
  Pallas kernels  46.4 us (82%)
  local copies, waits for them, and re-layouts  9.08 us (16%)
  between operations  0.73 us (1%)
    pallas_call x1, Pallas kernels, shards(): pl.pallas_call(functools.partial(kernel, nz, ny), out_shape=(jax.ShapeDty...  46.4 us
    unnamed x16, local copies, waits for them, and re-layouts  6.67 us

profile of v1, /device:TPU:1, one launch (start us, length us, event | category | flops | bytes accessed | tf_op | source)
XLA Modules:
  0.0 56.2 jit_solution(4581372880237770329)
XLA Ops:
  0.6 0.0 copy-start.3
  0.6 0.0 copy-start.2
  0.7 0.0 copy-start.1
  0.7 0.0 copy-start
  0.7 0.8 %reshape.13.gain = f32[1,384]{1,0:T(1,128)S(1)} reshape(f32[384]{0:T(512)} %param.12) | data formatting | bytes 3072 | tf_op jit(solution)/shard_map/reshape | solution.py:504
  1.4 0.7 %reshape.14.attn_gain = f32[1,384]{1,0:T(1,128)S(1)} reshape(f32[384]{0:T(512)} %param.14) | data formatting | bytes 3072 | tf_op jit(solution)/shard_map/reshape | solution.py:504
  2.1 2.5 %copy.12.up_hbm = bf16[3,3,384,192]{3,2,1,0:T(8,128)(2,1)S(1)} copy(bf16[3,3,384,192]{2,3,1,0:T(8,128)(2,1)} %param.19) | data formatting | bytes 2654208 | tf_op args[9]
  4.7 0.0 copy-done.3
  4.7 0.0 copy-done.2
  4.7 0.0 copy-done.1
  4.7 0.0 copy-done
  4.7 0.0 copy-start.5
  4.7 0.9 %copy-done.5 = bf16[2,2,64,384]{3,2,1,0:T(8,128)(2,1)S(1)} copy-done((bf16[2,2,64,384]{3,2,1,0:T(8,128)(2,1)S(1)}, bf16[2,2,64,384]{3,2,1,0:T(8,128)(2,1)}, u32[]{:S(2)}) %copy-start.5) | copy-done | bytes 196632
  5.6 0.0 copy-start.6
  5.6 0.9 %copy-done.6 = bf16[2,2,64,384]{3,2,1,0:T(8,128)(2,1)S(1)} copy-done((bf16[2,2,64,384]{3,2,1,0:T(8,128)(2,1)S(1)}, bf16[2,2,64,384]{3,2,1,0:T(8,128)(2,1)}, u32[]{:S(2)}) %copy-start.6) | copy-done | bytes 196632
  6.6 46.4 %shard_map.113 = (bf16[2,4,128,192]{3,2,1,0:T(8,128)(2,1)S(1)}, bf16[2,2,64,384]{3,2,1,0:T(8,128)(2,1)S(1)}) custom-call(bf16[2,2,64,384]{3,2,1,0:T(8,128)(2,1)S(1)} %copy-done.5, bf16[2,2,64,384]{3,2,1,0:T(8,128)(2,1)S(1)} %copy-done.6, f32[1,384]{1,0:T(1,128)S(1)} %reshape.13.gain, f32[1,384]{1,0:T(1,128)S(1)} %reshape.14.attn_gain, ...), custom_call_target="tpu_custom_call" | custom-call | tf_op jit(solution)/shard_map/pallas_call | solution.py:469
  53.0 0.0 copy-start.4
  53.0 0.7 %copy-done.4 = bf16[2,2,64,384]{3,2,1,0:T(8,128)(2,1)} copy-done((bf16[2,2,64,384]{3,2,1,0:T(8,128)(2,1)}, bf16[2,2,64,384]{3,2,1,0:T(8,128)(2,1)S(1)}, u32[]{:S(2)}) %copy-start.4) | copy-done | bytes 196632
  53.6 1.0 %copy.13 = bf16[2,4,128,192]{2,3,1,0:T(8,128)(2,1)} copy(bf16[2,4,128,192]{3,2,1,0:T(8,128)(2,1)S(1)} %get-tuple-element.2) | data formatting | bytes 786432 | tf_op jit(solution)/shard_map/pallas_call | solution.py:469
  54.6 1.6 %copy.15 = bf16[2,2,64,384]{3,2,1,0:T(8,128)(2,1)} copy(bf16[2,2,64,384]{3,2,1,0:T(8,128)(2,1)} %copy-done.4) | data formatting | bytes 393216
Async XLA Ops:
  0.6 4.0 %copy-start.3 = (bf16[384,384]{1,0:T(8,128)(2,1)S(1)}, bf16[384,384]{1,0:T(8,128)(2,1)}, u32[]{:S(2)}) copy-start(bf16[384,384]{1,0:T(8,128)(2,1)} %o_hbm.1) | copy-start | bytes 884740
  0.6 4.0 %copy-start.2 = (bf16[384,384]{1,0:T(8,128)(2,1)S(1)}, bf16[384,384]{1,0:T(8,128)(2,1)}, u32[]{:S(2)}) copy-start(bf16[384,384]{1,0:T(8,128)(2,1)} %v_hbm.1) | copy-start | bytes 884740
  0.7 4.0 %copy-start.1 = (bf16[384,384]{1,0:T(8,128)(2,1)S(1)}, bf16[384,384]{1,0:T(8,128)(2,1)}, u32[]{:S(2)}) copy-start(bf16[384,384]{1,0:T(8,128)(2,1)} %k_hbm.1) | copy-start | bytes 884740
  0.7 4.0 %copy-start = (bf16[384,384]{1,0:T(8,128)(2,1)S(1)}, bf16[384,384]{1,0:T(8,128)(2,1)}, u32[]{:S(2)}) copy-start(bf16[384,384]{1,0:T(8,128)(2,1)} %q_hbm.1) | copy-start | bytes 884740
  4.7 0.9 %copy-start.5 = (bf16[2,2,64,384]{3,2,1,0:T(8,128)(2,1)S(1)}, bf16[2,2,64,384]{3,2,1,0:T(8,128)(2,1)}, u32[]{:S(2)}) copy-start(bf16[2,2,64,384]{3,2,1,0:T(8,128)(2,1)} %latents.1) | copy-start | bytes 589828
  5.6 0.9 %copy-start.6 = (bf16[2,2,64,384]{3,2,1,0:T(8,128)(2,1)S(1)}, bf16[2,2,64,384]{3,2,1,0:T(8,128)(2,1)}, u32[]{:S(2)}) copy-start(bf16[2,2,64,384]{3,2,1,0:T(8,128)(2,1)} %cache.1) | copy-start | bytes 589828
  53.0 0.7 %copy-start.4 = (bf16[2,2,64,384]{3,2,1,0:T(8,128)(2,1)}, bf16[2,2,64,384]{3,2,1,0:T(8,128)(2,1)S(1)}, u32[]{:S(2)}) copy-start(bf16[2,2,64,384]{3,2,1,0:T(8,128)(2,1)S(1)} %get-tuple-element.7) | copy-start | bytes 589828

commit v2 on v1

--- a/solution.py
+++ b/solution.py
@@ -33,9 +33,9 @@
 
 def kernel(
     nz, ny,
-    latents, cache, gain, attn_gain, conv_hbm, q_hbm, k_hbm, v_hbm, o_hbm, up_hbm,
+    latents_hbm, cache_hbm, gain, attn_gain, conv_hbm, q_hbm, k_hbm, v_hbm, o_hbm, up_hbm,
     decoded, next_cache,
-    conv_w, q_w, k_w, v_w, o_w, up_w, up_p,
+    latents, wide, conv_w, q_w, k_w, v_w, o_w, up_w, up_p,
     lat, stk, ext, ext3, resid, keys, query, top, total, acc, mid, midx, mid3,
     w_sem, a_send, a_recv, z_send, z_recv, y_send, y_recv, c_send, c_recv,
 ):
@@ -49,6 +49,10 @@
     sibling = me + 1 - 2 * core
     has_prev, has_next = chip > 0, chip < chips - 1
 
+    latents_in = pltpu.make_async_copy(latents_hbm, latents, w_sem.at[8])
+    cache_in = pltpu.make_async_copy(cache_hbm, stk.at[pl.ds(0, 2)], w_sem.at[9])
+    latents_in.start()
+    cache_in.start()
     weights = [
         pltpu.make_async_copy(conv_hbm.at[pl.ds(3 * i, 3)], conv_w.at[pl.ds(3 * i, 3)], w_sem.at[i])
         for i in range(3)
@@ -103,13 +107,8 @@
             device_id_type=pl.DeviceIdType.MESH,
         )
 
-    values_in = latents[...].astype(F32)
-    normal = normalize(values_in, gain[...].reshape(1, 1, 1, channels))
-    conv_input = (normal / (1.0 + jnp.exp(-normal))).astype(BF16)
-    next_cache[...] = conv_input
-    stk[0:2] = cache[...]
-    stk[2:4] = conv_input
-
+    cache_in.wait()
+    latents_in.wait()
     pl.semaphore_wait(barrier, met)
 
     def halo(group, first, count, slot, source_row, target_row, device, kind):
@@ -148,18 +147,28 @@
     sends_down = (core == 1) & has_next
     sends_up = (core == 0) & has_prev
 
-    @pl.when(sends_down)
-    def _():
-        for copy in down_halo:
-            copy.start()
-
-    @pl.when(sends_up)
-    def _():
-        for copy in up_halo:
-            copy.start()
-
-    for copy in to_sibling:
-        copy.start()
+    def start_halos(step):
+        @pl.when(sends_down)
+        def _():
+            for copy in down_halo[2 * step : 2 * step + 2]:
+                copy.start()
+
+        @pl.when(sends_up)
+        def _():
+            for copy in up_halo[2 * step : 2 * step + 2]:
+                copy.start()
+
+    start_halos(0)
+    to_sibling[0].start()
+    to_sibling[2].start()
+    normal = normalize(latents[...].astype(F32), gain[...].reshape(1, 1, 1, channels))
+    conv_input = (normal / (1.0 + jnp.exp(-normal))).astype(BF16)
+    stk[2:4] = conv_input
+    start_halos(1)
+    to_sibling[1].start()
+    wide[...] = conv_input.astype(F32)
+    cache_out = pltpu.make_async_copy(wide, next_cache, w_sem.at[10])
+    cache_out.start()
 
     ext[:, pl.ds(1 + rows * core, rows)] = stk[pl.ds(core, 3)]
     lat[pl.ds(rows * core, rows)] = latents[core]
@@ -200,41 +209,36 @@
     arrived(lat.at[pl.ds(rows * other, rows)], a_recv.at[2])
     resid_now = lat[...].reshape(band * width, channels).astype(F32) + conv_out
     resid[...] = resid_now
-    normed = normalize(resid_now, attn_gain[...]).astype(BF16)
+    normed = normalize(resid_now, attn_gain[...].reshape(1, channels)).astype(BF16)
     keys[chip] = normed
 
-    def up(block):
-        index = block * ny + y
-        return remote(
-            keys.at[index], keys.at[index], z_send.at[block], z_recv.at[block], me + 2 * ny
-        )
-
-    def down(block):
-        index = block * ny + y
-        return remote(
-            keys.at[index], keys.at[index], z_send.at[nz + block], z_recv.at[block], me - 2 * ny
-        )
-
-    def across(block):
-        index = block * ny + y
-        return remote(
-            keys.at[index],
-            keys.at[index],
-            y_send.at[block],
-            y_recv.at[block],
-            me + 2 * (1 - 2 * y),
-        )
-
-    @pl.when(z < nz - 1)
-    def _():
-        up(z).start()
-
-    @pl.when(z > 0)
-    def _():
-        down(z).start()
-
-    if ny > 1:
-        across(z).start()
+    def piece(index, row):
+        return keys.at[index, pl.ds(row * width, width)]
+
+    def up(block, row):
+        part = piece(block * ny + y, row)
+        return remote(part, part, z_send.at[block], z_recv.at[block, row], me + 2 * ny)
+
+    def down(block, row):
+        part = piece(block * ny + y, row)
+        return remote(part, part, z_send.at[nz + block], z_recv.at[block, row], me - 2 * ny)
+
+    def across(block, row):
+        part = piece(block * ny + y, row)
+        return remote(part, part, y_send.at[block], y_recv.at[block], me + 2 * (1 - 2 * y))
+
+    for row in range(band):
+
+        @pl.when(z < nz - 1)
+        def _():
+            up(z, row).start()
+
+        @pl.when(z > 0)
+        def _():
+            down(z, row).start()
+
+        if ny > 1:
+            across(z, row).start()
 
     for copy in weights[3:]:
         copy.wait()
@@ -258,7 +262,7 @@
                         for l in taps[l_sets, u]:
                             term = up_w[j, l].astype(F32)
                             summed = term if summed is None else summed + term
-                    up_p[a, l_sets, t, u * channels : (u + 1) * channels] = summed.astype(BF16)
+                    up_p[a, l_sets, t, :, u * channels : (u + 1) * channels] = summed.astype(BF16)
 
     def attend(index):
         block = keys[index]
@@ -271,62 +275,72 @@
         total[...] = total[...] * fade + jnp.sum(part, axis=-1, keepdims=True)
         acc[...] = acc[...] * fade + dot(part.astype(BF16), block)
 
-    def z_arrived(block):
-        index = block * ny + y
-        remote(keys.at[index], keys.at[index], z_send.at[0], z_recv.at[block], sibling).wait_recv()
-
-    def y_arrived(block):
-        index = block * ny + 1 - y
-        remote(keys.at[index], keys.at[index], y_send.at[0], y_recv.at[block], sibling).wait_recv()
+    def z_arrived(block, row):
+        part = piece(block * ny + y, row)
+        remote(part, part, z_send.at[0], z_recv.at[block, row], sibling).wait_recv()
+
+    def attend_z(block):
+        @pl.when((block >= 0) & (block < nz))
+        def _():
+            attend(block * ny + y)
+
+    def attend_y(block):
+        if ny > 1:
+
+            @pl.when((block >= 0) & (block < nz))
+            def _():
+                whole = keys.at[block * ny + 1 - y]
+                remote(whole, whole, y_send.at[0], y_recv.at[block], sibling).wait_recv()
+                attend(block * ny + 1 - y)
 
     def gather_step(d, carry):
         low, high = z - d, z + d
-
-        @pl.when(low >= 0)
-        def _():
-            z_arrived(low)
-
-            @pl.when(z < nz - 1)
+        late_low = jnp.where(d > 1, low + 1, -1)
+        late_high = jnp.where(d > 1, high - 1, nz)
+        across_low = jnp.where(d > 1, low + 2, -1)
+        across_high = jnp.where(d > 2, high - 2, nz)
+        for row in range(band):
+
+            @pl.when(low >= 0)
             def _():
-                up(low).start()
-
-            if ny > 1:
-                across(low).start()
-
-        @pl.when(high < nz)
-        def _():
-            z_arrived(high)
-
-            @pl.when(z > 0)
+                z_arrived(low, row)
+
+                @pl.when(z < nz - 1)
+                def _():
+                    up(low, row).start()
+
+                if ny > 1:
+                    across(low, row).start()
+
+            @pl.when(high < nz)
             def _():
-                down(high).start()
-
-            if ny > 1:
-                across(high).start()
-
-        @pl.when(low >= 0)
-        def _():
-            attend(low * ny + y)
-
-        @pl.when(high < nz)
-        def _():
-            attend(high * ny + y)
-
-        if ny > 1:
-
-            @pl.when(low + 1 >= 0)
-            def _():
-                y_arrived(low + 1)
-                attend((low + 1) * ny + 1 - y)
-
-            @pl.when((high - 1 < nz) & (d > 1))
-            def _():
-                y_arrived(high - 1)
-                attend((high - 1) * ny + 1 - y)
+                z_arrived(high, row)
+
+                @pl.when(z > 0)
+                def _():
+                    down(high, row).start()
+
+                if ny > 1:
+                    across(high, row).start()
+
+            if row == 0:
+                attend_z(late_low)
+            elif row == 1:
+                attend_z(late_high)
+            elif row == 2:
+                attend_y(across_low)
+            else:
+                attend_y(across_high)
 
         return carry
 
-    lax.fori_loop(1, nz + 1 if ny > 1 else nz, gather_step, 0)
+    lax.fori_loop(1, nz, gather_step, 0)
+    attend_z(z - nz + 1)
+    attend_z(z + nz - 1)
+    attend_y(z - nz + 2)
+    attend_y(jnp.where(nz > 2, z + nz - 2, nz))
+    attend_y(z - nz + 1)
+    attend_y(z + nz - 1)
 
     mixed = (acc[...] / total[...]).astype(BF16)
     attended = dot(mixed, v_w[...]).astype(BF16)
@@ -387,21 +401,22 @@
             copy.wait_send()
 
     def sent(block, carry):
+        whole = keys.at[block * ny + y]
+
         @pl.when((block <= z) & (z < nz - 1))
         def _():
-            up(block).wait_send()
+            remote(whole, whole, z_send.at[block], z_recv.at[0, 0], sibling).wait_send()
 
         @pl.when((block >= z) & (z > 0))
         def _():
-            down(block).wait_send()
+            remote(whole, whole, z_send.at[nz + block], z_recv.at[0, 0], sibling).wait_send()
 
         if ny > 1:
-            across(block).wait_send()
+            remote(whole, whole, y_send.at[block], y_recv.at[0], sibling).wait_send()
         return carry
 
     lax.fori_loop(0, nz, sent, 0)
 
-    target = midx.at[other, pl.ds(core, near)]
     remote(
         midx.at[other, pl.ds(1 - core, near)],
         midx.at[other, pl.ds(1 - core, near)],
@@ -432,7 +447,7 @@
                     :, (a + t) * width : (a + t + rows) * width,
                     b * channels : (b + 2) * channels,
                 ].reshape(2 * rows * width, 2 * channels)
-                term = dot(window, up_p[a, b, t])
+                term = dot_nt(window, up_p[a, b, t])
                 result = term if result is None else result + term
             sides.append(result.astype(BF16).reshape(2, rows, width, outputs))
         for f in range(2):
@@ -440,6 +455,7 @@
                 pair = jnp.concatenate([sides[0][f, r], sides[1][f, r]], axis=0)
                 decoded[f, 2 * r + a] = dot(weave, pair).astype(BF16)
 
+    cache_out.wait()
     mid_sibling.wait_send()
 
     @pl.when(has_next)
@@ -463,22 +479,24 @@
         outputs = up_weight.shape[3]
         band = 2 * rows
         vmem = pl.BlockSpec(memory_space=pltpu.VMEM)
-        hbm = pl.BlockSpec(memory_space=pl.ANY)
+        hbm = pl.BlockSpec(memory_space=pltpu.HBM)
         square = pltpu.VMEM((channels, channels), BF16)
         dma = pltpu.SemaphoreType.DMA
-        return pl.pallas_call(
+        decoded, next_cache = pl.pallas_call(
             functools.partial(kernel, nz, ny),
             out_shape=(
                 jax.ShapeDtypeStruct((frames, 2 * rows, 2 * width, outputs), BF16),
-                jax.ShapeDtypeStruct(latents.shape, BF16),
+                jax.ShapeDtypeStruct(latents.shape, F32),
             ),
-            in_specs=[vmem] * 4 + [hbm] * 6,
-            out_specs=(vmem, vmem),
+            in_specs=[hbm] * 2 + [vmem] * 2 + [hbm] * 6,
+            out_specs=(vmem, hbm),
             scratch_shapes=[
+                pltpu.VMEM(latents.shape, BF16),
+                pltpu.VMEM(latents.shape, F32),
                 pltpu.VMEM((9, 3 * channels, channels), BF16),
                 square, square, square, square,
-                pltpu.VMEM((3, 3, channels, outputs), BF16),
-                pltpu.VMEM((2, 2, 2, 2 * channels, outputs), BF16),
+                pltpu.VMEM((3, 3, outputs, channels), BF16),
+                pltpu.VMEM((2, 2, 2, outputs, 2 * channels), BF16),
                 pltpu.VMEM((band, width, channels), BF16),
                 pltpu.VMEM((4, rows, width, channels), BF16),
                 pltpu.VMEM((3, band + 2, width, channels), BF16),
@@ -492,19 +510,20 @@
                 pltpu.VMEM((band, width, channels), BF16),
                 pltpu.VMEM((2, rows + 2, width, channels), BF16),
                 pltpu.VMEM((2, (rows + 2) * width, 3 * channels), BF16),
-                dma((8,)), dma((7,)), dma((7,)),
-                dma((2 * nz,)), dma((nz,)), dma((nz,)), dma((nz,)),
+                dma((11,)), dma((7,)), dma((7,)),
+                dma((2 * nz,)), dma((nz, band)), dma((nz,)), dma((nz,)),
                 dma((3,)), dma((3,)),
             ],
             compiler_params=pltpu.CompilerParams(
-                collective_id=0, has_side_effects=True, vmem_limit_bytes=50 * 1024 * 1024
+                collective_id=0, has_side_effects=True, vmem_limit_bytes=60 * 1024 * 1024
             ),
         )(
             latents, conv_cache,
-            norm_gain.reshape(1, channels), attn_gain.reshape(1, channels),
+            norm_gain, attn_gain,
             conv_weight.reshape(9, 3 * channels, channels),
-            query_weight, key_weight, value_weight, out_weight, up_weight,
+            query_weight, key_weight, value_weight, out_weight, up_weight.swapaxes(2, 3),
         )
+        return decoded, next_cache.astype(BF16)
 
     split = P("videos", "rows", None, None)
     return jax.shard_map(

time: 56.5 us -> 44.4 us (0.79)
  local copies, waits for them, and re-layouts: 9.08 us -> 1.99 us
  Pallas kernels: 46.4 us -> 39.5 us
  other arithmetic: 0 us -> 1.7 us
    pallas_call x1, Pallas kernels: 46.4 us -> 39.5 us  [shards(): pl.pallas_call(functools.partial(kernel, nz, ny), out_shape=(jax.ShapeDty...]
    unnamed x16 -> x1, local copies, waits for them, and re-layouts: 6.67 us -> 1.99 us
    convert_element_type x0 -> x1, other arithmetic: none -> 1.7 us  [shards(): return (decoded, next_cache.astype(BF16))]
    reshape x2 -> x0, local copies, waits for them, and re-layouts: 1.46 us -> none  [the longest x1 0.77 us: shards(): norm_gain.reshape(1, channels)]
    pallas_call x1 -> x0, local copies, waits for them, and re-layouts: 0.95 us -> none  [shards(): pl.pallas_call(functools.partial(kernel, nz, ny), out_shape=(jax.ShapeDty...]
where the time goes in v2:
time: 44.4 us; the launch traced here: 43.8 us
  Pallas kernels  39.5 us (89%)
  local copies, waits for them, and re-layouts  1.99 us (4%)
  other arithmetic  1.7 us (4%)
  between operations  0.64 us (1%)
    pallas_call x1, Pallas kernels, shards(): pl.pallas_call(functools.partial(kernel, nz, ny), out_shape=(jax.ShapeDty...  39.5 us
    unnamed x1, local copies, waits for them, and re-layouts  1.99 us
    convert_element_type x1, other arithmetic, shards(): return (decoded, next_cache.astype(BF16))  1.7 us

profile of v2, /device:TPU:1, one launch (start us, length us, event | category | flops | bytes accessed | tf_op | source)
XLA Modules:
  0.0 43.8 jit_solution(4524118226730456674)
XLA Ops:
  0.6 39.5 %shard_map.113 = (bf16[2,4,128,192]{3,2,1,0:T(8,128)(2,1)}, f32[2,2,64,384]{3,2,1,0:T(8,128)}) custom-call(bf16[2,2,64,384]{3,2,1,0:T(8,128)(2,1)} %latents_hbm.1, bf16[2,2,64,384]{3,2,1,0:T(8,128)(2,1)} %cache_hbm.1, f32[384]{0:T(512)} %gain.1, f32[384]{0:T(512)} %attn_gain.1, bf16[9,1152,384]{2,1,0:T(8,128)(2,1)} %bitcast.2, bf16[384,384]{1,0:T(8,128)(2,1)} %q_hbm.1, ...), custom_call_target="tpu_custom_call" | custom-call | tf_op jit(solution)/shard_map/pallas_call | solution.py:485
  40.1 2.0 %copy.12 = bf16[2,4,128,192]{2,3,1,0:T(8,128)(2,1)} copy(bf16[2,4,128,192]{3,2,1,0:T(8,128)(2,1)} %get-tuple-element.6) | data formatting | bytes 786432
  42.1 1.7 %convert_element_type.3 = bf16[2,2,64,384]{3,2,1,0:T(8,128)(2,1)} convert(f32[2,2,64,384]{3,2,1,0:T(8,128)} %get-tuple-element.5) | non-fusion elementwise | flops 98304 | bytes 589824 | tf_op jit(solution)/shard_map/convert_element_type | solution.py:526

commit v3 on v2

--- a/solution.py
+++ b/solution.py
@@ -35,13 +35,13 @@
     nz, ny,
     latents_hbm, cache_hbm, gain, attn_gain, conv_hbm, q_hbm, k_hbm, v_hbm, o_hbm, up_hbm,
     decoded, next_cache,
-    latents, wide, conv_w, q_w, k_w, v_w, o_w, up_w, up_p,
-    lat, stk, ext, ext3, resid, keys, query, top, total, acc, mid, midx, mid3,
+    conv_w, q_w, k_w, v_w, o_w, up_w, up_p,
+    stk, own, ext, ext3, resid, keys, query, top, total, acc, mid, midx, mid3,
     w_sem, a_send, a_recv, z_send, z_recv, y_send, y_recv, c_send, c_recv,
 ):
-    _, rows, width, channels = latents.shape
+    _, rows, width, channels = latents_hbm.shape
     band = 2 * rows
-    outputs = decoded.shape[3]
+    outputs = decoded.shape[2]
     me = lax.axis_index("rows")
     chip, core = me // 2, me % 2
     z, y = chip // ny, chip % ny
@@ -49,7 +49,7 @@
     sibling = me + 1 - 2 * core
     has_prev, has_next = chip > 0, chip < chips - 1
 
-    latents_in = pltpu.make_async_copy(latents_hbm, latents, w_sem.at[8])
+    latents_in = pltpu.make_async_copy(latents_hbm, stk.at[pl.ds(2, 2)], w_sem.at[8])
     cache_in = pltpu.make_async_copy(cache_hbm, stk.at[pl.ds(0, 2)], w_sem.at[9])
     latents_in.start()
     cache_in.start()
@@ -111,67 +111,67 @@
     latents_in.wait()
     pl.semaphore_wait(barrier, met)
 
-    def halo(group, first, count, slot, source_row, target_row, device, kind):
-        return remote(
-            stk.at[pl.ds(group + first, count), pl.ds(source_row, 1)],
-            ext.at[pl.ds(first, count), pl.ds(target_row, 1)],
-            a_send.at[slot],
-            a_recv.at[kind],
-            device,
-        )
-
     other = 1 - core
+    pair = core
+    third = 2 - 2 * core
+    others_pair = other
+    others_third = 2 - 2 * other
+    mine = pl.ds(1 + rows * core, rows)
+    siblings = pl.ds(1 + rows * other, rows)
+    above, below = pl.ds(0, 1), pl.ds(band + 1, 1)
     to_sibling = [
         remote(
-            stk.at[pl.ds(other + first, count)],
-            ext.at[pl.ds(first, count), pl.ds(1 + rows * core, rows)],
-            a_send.at[slot],
-            a_recv.at[slot],
-            sibling,
+            stk.at[pl.ds(2 * other, 2)],
+            ext.at[pl.ds(others_pair, 2), mine],
+            a_send.at[0], a_recv.at[0], sibling,
+        ),
+        remote(
+            stk.at[pl.ds(2 - other, 1)],
+            ext.at[pl.ds(others_third, 1), mine],
+            a_send.at[1], a_recv.at[1], sibling,
+        ),
+    ]
+    down_halo = [
+        remote(
+            stk.at[pl.ds(2 * g, 2), pl.ds(rows - 1, 1)],
+            ext.at[pl.ds(g, 2), above],
+            a_send.at[2 + g], a_recv.at[2], 2 * chip + 2 + g,
         )
-        for slot, (first, count) in enumerate(((0, 1), (1, 2)))
+        for g in range(2)
     ]
-    to_sibling.append(
+    up_halo = [
         remote(
-            latents.at[other], lat.at[pl.ds(rows * core, rows)], a_send.at[2], a_recv.at[2], sibling
+            stk.at[pl.ds(2 * g, 2), pl.ds(0, 1)],
+            ext.at[pl.ds(g, 2), below],
+            a_send.at[2 + g], a_recv.at[4], 2 * chip - 2 + g,
         )
-    )
-    up_halo, down_halo = [], []
-    for step, (first, count) in enumerate(((0, 1), (1, 2))):
-        for g in range(2):
-            slot = 3 + 2 * step + g
-            down_halo.append(
-                halo(g, first, count, slot, rows - 1, 0, 2 * chip + 2 + g, 3 + step)
-            )
-            up_halo.append(halo(g, first, count, slot, 0, band + 1, 2 * chip - 2 + g, 5 + step))
+        for g in range(2)
+    ]
+    pass_above, pass_below = [
+        remote(
+            ext.at[pl.ds(1, 1), row],
+            ext.at[pl.ds(others_third, 1), row],
+            a_send.at[4 + i], a_recv.at[3 + 2 * i], sibling,
+        )
+        for i, row in enumerate((above, below))
+    ]
     sends_down = (core == 1) & has_next
     sends_up = (core == 0) & has_prev
 
-    def start_halos(step):
-        @pl.when(sends_down)
-        def _():
-            for copy in down_halo[2 * step : 2 * step + 2]:
-                copy.start()
-
-        @pl.when(sends_up)
-        def _():
-            for copy in up_halo[2 * step : 2 * step + 2]:
-                copy.start()
-
-    start_halos(0)
-    to_sibling[0].start()
-    to_sibling[2].start()
-    normal = normalize(latents[...].astype(F32), gain[...].reshape(1, 1, 1, channels))
-    conv_input = (normal / (1.0 + jnp.exp(-normal))).astype(BF16)
-    stk[2:4] = conv_input
-    start_halos(1)
-    to_sibling[1].start()
-    wide[...] = conv_input.astype(F32)
-    cache_out = pltpu.make_async_copy(wide, next_cache, w_sem.at[10])
-    cache_out.start()
-
-    ext[:, pl.ds(1 + rows * core, rows)] = stk[pl.ds(core, 3)]
-    lat[pl.ds(rows * core, rows)] = latents[core]
+    @pl.when(sends_down)
+    def _():
+        for copy in down_halo:
+            copy.start()
+
+    @pl.when(sends_up)
+    def _():
+        for copy in up_halo:
+            copy.start()
+
+    for copy in to_sibling:
+        copy.start()
+
+    ext[:, mine] = stk[pl.ds(core, 3)]
     edge = jnp.zeros((3, 1, width, channels), BF16)
 
     @pl.when(jnp.logical_not(has_prev))
@@ -185,29 +185,56 @@
     def arrived(target, sem):
         remote(target, target, a_send.at[0], sem, sibling).wait_recv()
 
+    def activate(values):
+        normal = normalize(values.astype(F32), gain[...].reshape(1, channels))
+        return (normal / (1.0 + jnp.exp(-normal))).astype(BF16)
+
     conv_out = jnp.zeros((band * width, channels), F32)
     for i in range(3):
-        if i < 2:
-            first, count = ((0, 1), (1, 2))[i]
-            arrived(ext.at[pl.ds(first, count), pl.ds(1 + rows * other, rows)], a_recv.at[i])
+        t = lax.rem(i + core, 3)
+        if i == 0:
 
             @pl.when(has_prev)
             def _():
-                arrived(ext.at[pl.ds(first, count), pl.ds(0, 1)], a_recv.at[3 + i])
+                arrived(ext.at[pl.ds(pair, 2), above], a_recv.at[2])
+                pass_above.start()
 
             @pl.when(has_next)
             def _():
-                arrived(ext.at[pl.ds(first, count), pl.ds(band + 1, 1)], a_recv.at[5 + i])
-
-        flat = ext[i].reshape((band + 2) * width, channels)
-        ext3[i] = with_columns(flat, width)
-        weights[i].wait()
+                arrived(ext.at[pl.ds(pair, 2), below], a_recv.at[4])
+                pass_below.start()
+
+            arrived(ext.at[pl.ds(pair, 2), siblings], a_recv.at[0])
+        if i == 2:
+            arrived(ext.at[pl.ds(third, 1), siblings], a_recv.at[1])
+
+            @pl.when(has_prev)
+            def _():
+                arrived(ext.at[pl.ds(third, 1), above], a_recv.at[3])
+
+            @pl.when(has_next)
+            def _():
+                arrived(ext.at[pl.ds(third, 1), below], a_recv.at[5])
+
+        fresh = core == (0 if i == 2 else 1)
+
+        @pl.when(fresh)
+        def _():
+            flat = ext[t].reshape((band + 2) * width, channels)
+            ext3[i] = with_columns(activate(flat), width)
+
+        @pl.when(jnp.logical_not(fresh))
+        def _():
+            ext3[i] = with_columns(ext[t].reshape((band + 2) * width, channels), width)
+
+        pltpu.make_async_copy(
+            conv_hbm.at[pl.ds(3 * t, 3)], conv_w.at[pl.ds(3 * t, 3)], w_sem.at[t]
+        ).wait()
         for j in range(3):
             window = ext3[i, j * width : (j + band) * width]
-            conv_out = conv_out + dot(window, conv_w[3 * i + j])
-
-    arrived(lat.at[pl.ds(rows * other, rows)], a_recv.at[2])
-    resid_now = lat[...].reshape(band * width, channels).astype(F32) + conv_out
+            conv_out = conv_out + dot(window, conv_w[3 * t + j])
+
+    resid_now = ext[2, 1 : 1 + band].reshape(band * width, channels).astype(F32) + conv_out
     resid[...] = resid_now
     normed = normalize(resid_now, attn_gain[...].reshape(1, channels)).astype(BF16)
     keys[chip] = normed
@@ -240,6 +267,9 @@
         if ny > 1:
             across(z, row).start()
 
+    own[...] = activate(stk[2:4].reshape(2 * rows * width, channels)).reshape(own.shape)
+    cache_out = pltpu.make_async_copy(own, next_cache, w_sem.at[10])
+    cache_out.start()
     for copy in weights[3:]:
         copy.wait()
     queries = dot(normed, q_w[...]).astype(BF16)
@@ -390,6 +420,14 @@
     for copy in to_sibling:
         copy.wait_send()
 
+    @pl.when(has_prev)
+    def _():
+        pass_above.wait_send()
+
+    @pl.when(has_next)
+    def _():
+        pass_below.wait_send()
+
     @pl.when(sends_down)
     def _():
         for copy in down_halo:
@@ -453,7 +491,9 @@
         for f in range(2):
             for r in range(rows):
                 pair = jnp.concatenate([sides[0][f, r], sides[1][f, r]], axis=0)
-                decoded[f, 2 * r + a] = dot(weave, pair).astype(BF16)
+                decoded[f, 2 * r + a] = lax.dot_general(
+                    pair, weave, (((0,), (1,)), ((), ())), preferred_element_type=F32
+                ).astype(BF16)
 
     cache_out.wait()
     mid_sibling.wait_send()
@@ -465,6 +505,11 @@
     @pl.when(has_prev)
     def _():
         mid_up.wait_send()
+
+
+def finish(decoded_in, cache_in, decoded, next_cache):
+    decoded[...] = decoded_in[...]
+    next_cache[...] = cache_in[...]
 
 
 def solution(mesh):
@@ -485,20 +530,18 @@
         decoded, next_cache = pl.pallas_call(
             functools.partial(kernel, nz, ny),
             out_shape=(
-                jax.ShapeDtypeStruct((frames, 2 * rows, 2 * width, outputs), BF16),
-                jax.ShapeDtypeStruct(latents.shape, F32),
+                jax.ShapeDtypeStruct((frames, 2 * rows, outputs, 2 * width), BF16),
+                jax.ShapeDtypeStruct(latents.shape, BF16),
             ),
             in_specs=[hbm] * 2 + [vmem] * 2 + [hbm] * 6,
             out_specs=(vmem, hbm),
             scratch_shapes=[
-                pltpu.VMEM(latents.shape, BF16),
-                pltpu.VMEM(latents.shape, F32),
                 pltpu.VMEM((9, 3 * channels, channels), BF16),
                 square, square, square, square,
                 pltpu.VMEM((3, 3, outputs, channels), BF16),
                 pltpu.VMEM((2, 2, 2, outputs, 2 * channels), BF16),
-                pltpu.VMEM((band, width, channels), BF16),
                 pltpu.VMEM((4, rows, width, channels), BF16),
+                pltpu.VMEM(latents.shape, BF16),
                 pltpu.VMEM((3, band + 2, width, channels), BF16),
                 pltpu.VMEM((3, (band + 2) * width, 3 * channels), BF16),
                 pltpu.VMEM((band * width, channels), F32),
@@ -510,7 +553,7 @@
                 pltpu.VMEM((band, width, channels), BF16),
                 pltpu.VMEM((2, rows + 2, width, channels), BF16),
                 pltpu.VMEM((2, (rows + 2) * width, 3 * channels), BF16),
-                dma((11,)), dma((7,)), dma((7,)),
+                dma((11,)), dma((6,)), dma((6,)),
                 dma((2 * nz,)), dma((nz, band)), dma((nz,)), dma((nz,)),
                 dma((3,)), dma((3,)),
             ],
@@ -523,7 +566,16 @@
             conv_weight.reshape(9, 3 * channels, channels),
             query_weight, key_weight, value_weight, out_weight, up_weight.swapaxes(2, 3),
         )
-        return decoded, next_cache.astype(BF16)
+        decoded, next_cache = pl.pallas_call(
+            finish,
+            out_shape=(
+                jax.ShapeDtypeStruct(decoded.shape, BF16),
+                jax.ShapeDtypeStruct(next_cache.shape, BF16),
+            ),
+            in_specs=[vmem] * 2,
+            out_specs=(vmem, vmem),
+        )(decoded, next_cache)
+        return decoded.swapaxes(2, 3), next_cache
 
     split = P("videos", "rows", None, None)
     return jax.shard_map(

time: 44.4 us -> 41.7 us (0.939)
  local copies, waits for them, and re-layouts: 1.99 us -> 0 us
  other arithmetic: 1.7 us -> 0 us
  Pallas kernels: 39.5 us -> 40.7 us
    unnamed x1 -> x0, local copies, waits for them, and re-layouts: 1.99 us -> none
    pallas_call x0 -> x1, Pallas kernels: none -> 1.88 us  [shards(): pl.pallas_call(finish, out_shape=(jax.ShapeDtypeStruct(decoded.shape, BF1...]
    convert_element_type x1 -> x0, other arithmetic: 1.7 us -> none  [shards(): return (decoded, next_cache.astype(BF16))]
    pallas_call x1, Pallas kernels: 39.5 us -> 38.8 us  [shards(): pl.pallas_call(functools.partial(kernel, nz, ny), out_shape=(jax.ShapeDty...]
where the time goes in v3:
time: 41.7 us; the launch traced here: 41.3 us
  Pallas kernels  40.7 us (98%)
  between operations  0.64 us (2%)
    pallas_call x1, Pallas kernels, shards(): pl.pallas_call(functools.partial(kernel, nz, ny), out_shape=(jax.ShapeDty...  38.8 us
    pallas_call x1, Pallas kernels, shards(): pl.pallas_call(finish, out_shape=(jax.ShapeDtypeStruct(decoded.shape, BF1...  1.88 us

profile of v3, /device:TPU:1, one launch (start us, length us, event | category | flops | bytes accessed | tf_op | source)
XLA Modules:
  0.0 41.3 jit_solution(11007822149138146725)
XLA Ops:
  0.6 38.8 %shard_map.113 = (bf16[2,4,192,128]{3,2,1,0:T(8,128)(2,1)}, bf16[2,2,64,384]{3,2,1,0:T(8,128)(2,1)}) custom-call(bf16[2,2,64,384]{3,2,1,0:T(8,128)(2,1)} %latents_hbm.1, bf16[2,2,64,384]{3,2,1,0:T(8,128)(2,1)} %cache_hbm.1, f32[384]{0:T(512)} %gain.1, f32[384]{0:T(512)} %attn_gain.1, bf16[9,1152,384]{2,1,0:T(8,128)(2,1)} %bitcast.3, bf16[384,384]{1,0:T(8,128)(2,1)} %q_hbm.1, ...), custom_call_target="tpu_custom_call" | custom-call | tf_op jit(solution)/shard_map/pallas_call | solution.py:530
  39.4 1.9 %shard_map.114 = (bf16[2,4,192,128]{3,2,1,0:T(8,128)(2,1)}, bf16[2,2,64,384]{3,2,1,0:T(8,128)(2,1)}) custom-call(bf16[2,4,192,128]{3,2,1,0:T(8,128)(2,1)} %get-tuple-element.6.decoded_in, bf16[2,2,64,384]{3,2,1,0:T(8,128)(2,1)} %get-tuple-element.7.cache_in), custom_call_target="tpu_custom_call" | custom-call | tf_op jit(solution)/shard_map/pallas_call | solution.py:569

commit v4 on v3

--- a/solution.py
+++ b/solution.py
@@ -267,9 +267,6 @@
         if ny > 1:
             across(z, row).start()
 
-    own[...] = activate(stk[2:4].reshape(2 * rows * width, channels)).reshape(own.shape)
-    cache_out = pltpu.make_async_copy(own, next_cache, w_sem.at[10])
-    cache_out.start()
     for copy in weights[3:]:
         copy.wait()
     queries = dot(normed, q_w[...]).astype(BF16)
@@ -283,16 +280,15 @@
     acc[...] = dot(part.astype(BF16), normed)
 
     taps = {(0, 0): (0,), (0, 1): (1, 2), (1, 0): (0, 1), (1, 1): (2,)}
-    for a in range(2):
-        for t in range(2):
-            for l_sets in range(2):
-                for u in range(2):
-                    summed = None
-                    for j in taps[a, t]:
-                        for l in taps[l_sets, u]:
-                            term = up_w[j, l].astype(F32)
-                            summed = term if summed is None else summed + term
-                    up_p[a, l_sets, t, :, u * channels : (u + 1) * channels] = summed.astype(BF16)
+    def add_taps(a, t):
+        for side in range(2):
+            for u in range(2):
+                summed = None
+                for j in taps[a, t]:
+                    for l in taps[side, u]:
+                        term = up_w[j, l].astype(F32)
+                        summed = term if summed is None else summed + term
+                up_p[a, side, t, :, u * channels : (u + 1) * channels] = summed.astype(BF16)
 
     def attend(index):
         block = keys[index]
@@ -361,6 +357,11 @@
                 attend_y(across_low)
             else:
                 attend_y(across_high)
+            if row < 4:
+
+                @pl.when(d == 1)
+                def _():
+                    add_taps(row // 2, row % 2)
 
         return carry
 
@@ -416,6 +417,10 @@
     @pl.when(jnp.logical_not(has_halo))
     def _():
         midx[:, pl.ds(edge_row, 1)] = jnp.zeros((2, 1, width, channels), BF16)
+
+    own[...] = activate(stk[2:4].reshape(2 * rows * width, channels)).reshape(own.shape)
+    cache_out = pltpu.make_async_copy(own, next_cache, w_sem.at[10])
+    cache_out.start()
 
     for copy in to_sibling:
         copy.wait_send()

time: 41.7 us -> 41.7 us (level)
  no operation moved by 1% of the time
where the time goes in v4:
time: 41.7 us; the launch traced here: 41.3 us
  Pallas kernels  40.7 us (98%)
  between operations  0.64 us (2%)
    pallas_call x1, Pallas kernels, shards(): pl.pallas_call(functools.partial(kernel, nz, ny), out_shape=(jax.ShapeDty...  38.8 us
    pallas_call x1, Pallas kernels, shards(): pl.pallas_call(finish, out_shape=(jax.ShapeDtypeStruct(decoded.shape, BF1...  1.88 us

profile of v4, /device:TPU:1, one launch (start us, length us, event | category | flops | bytes accessed | tf_op | source)
XLA Modules:
  0.0 41.3 jit_solution(12504257527875214173)
XLA Ops:
  0.6 38.8 %shard_map.113 = (bf16[2,4,192,128]{3,2,1,0:T(8,128)(2,1)}, bf16[2,2,64,384]{3,2,1,0:T(8,128)(2,1)}) custom-call(bf16[2,2,64,384]{3,2,1,0:T(8,128)(2,1)} %latents_hbm.1, bf16[2,2,64,384]{3,2,1,0:T(8,128)(2,1)} %cache_hbm.1, f32[384]{0:T(512)} %gain.1, f32[384]{0:T(512)} %attn_gain.1, bf16[9,1152,384]{2,1,0:T(8,128)(2,1)} %bitcast.3, bf16[384,384]{1,0:T(8,128)(2,1)} %q_hbm.1, ...), custom_call_target="tpu_custom_call" | custom-call | tf_op jit(solution)/shard_map/pallas_call | solution.py:535
  39.4 1.9 %shard_map.114 = (bf16[2,4,192,128]{3,2,1,0:T(8,128)(2,1)}, bf16[2,2,64,384]{3,2,1,0:T(8,128)(2,1)}) custom-call(bf16[2,4,192,128]{3,2,1,0:T(8,128)(2,1)} %get-tuple-element.6.decoded_in, bf16[2,2,64,384]{3,2,1,0:T(8,128)(2,1)} %get-tuple-element.7.cache_in), custom_call_target="tpu_custom_call" | custom-call | tf_op jit(solution)/shard_map/pallas_call | solution.py:574
